TPU v7x, 32 devices: a whole 2x2x4 slice. The times are simulated.
32 devices in a mesh: pipe: 16 (over z, y, core), tensor: 2 (over x).
Axes of the slice: x: 2, y: 2, z: 4, core: 2. Of those that a mesh axis runs over, the one named last changes fastest.
Arguments:
- up_weight: bfloat16 [16, 6400, 3200], P('pipe', 'tensor'), may hold values from -0.109375 to 0.109375
- down_weight: bfloat16 [16, 6400, 3200], P('pipe', 'tensor'), may hold values from -0.078125 to 0.078125
- norm_gain: float32 [16, 3200], P('pipe'), may hold values from 0.1 to 1.9
- layer_scale: float32 [16, 3200], P('pipe'), may hold values from 0.25 to 1
- stash: bfloat16 [16, 3, 256, 3200], P('pipe', None, 'tensor'), may hold values from -6 to 6
- slot_order: int32 [16, 3], P('pipe'), may hold values from 0 to 2, each once within a row
- received: float32 [16, 256, 3200], P('pipe', 'tensor'), may hold values from -6 to 6
- arrivals: bfloat16 [3, 64, 12800], P(None, 'tensor'), may hold values from -6 to 6
Outputs:
- emitted: bfloat16 [16, 3, 256, 3200], P('pipe', None, 'tensor')
- pending: float32 [16, 256, 3200], P('pipe', 'tensor')
Inputs may be any that keep to these rules, and one draw needn't show every extreme that they name: `slot_order`: each section's row is an ordering of the slots 0 to 2.
All inputs are finite; a program needn't handle non-finite values.
Results may differ from a plain program's by a relative error of at most 0.02.
Values may be sent and summed in bfloat16 or wider, within the bound.
A program may use at most 128 MiB of HBM per device.

v0:
```python
import functools

import jax
import jax.numpy as jnp
from jax import lax
from jax.experimental import pallas as pl
from jax.experimental.pallas import tpu as pltpu
from jax.sharding import PartitionSpec as P

GRID = 16
EPS = 1e-06
CHUNKS = 2
RING = CHUNKS
HELD = 2 * CHUNKS
TILE = 512
MESH = pl.DeviceIdType.MESH
NT = (((1,), (1,)), ((), ()))


def gelu_slope(hidden):
    return (
        0.5 * (1.0 + lax.erf(hidden * 0.7071067811865476))
        + hidden * jnp.exp(-0.5 * hidden * hidden) * 0.3989422804014327
    )


def tiles_of(size):
    return size // TILE, size % TILE


def kernel(
    n, sections, steps, order, gain, lscale, up_hbm, down_hbm, stash_hbm, received_hbm, landed_hbm,
    out_hbm, pend_hbm,
    up_w, down_w, stash, grads, landed, act, scaled, factor_of, slope, psend, precv, gin, moved_b,
    wsem, isem, a_send, a_recv, s_send, s_recv, p_send, p_recv, g_send, g_recv, o_sem, e_sem,
):
    hid, width = up_w.shape
    rows = grads.shape[1]
    me = lax.axis_index("tensor")
    sec = lax.axis_index("pipe")
    has_next = sec > 0
    has_prev = sec < sections - 1
    is_last = sec == sections - 1
    full, rem = tiles_of(hid)
    wfull, wrem = tiles_of(width)

    def peer(d):
        return lax.rem(me + d, n)

    in_stash = pltpu.make_async_copy(stash_hbm, stash, isem.at[0])
    in_grads = pltpu.make_async_copy(received_hbm, grads, isem.at[1])
    in_landed = pltpu.make_async_copy(landed_hbm, landed, isem.at[2])
    in_stash.start()
    in_grads.start()

    def weight_copies(j, size):
        first = j * TILE
        if not isinstance(j, int):
            first = pl.multiple_of(first, TILE)
        span = pl.ds(first, size)
        return (
            pltpu.make_async_copy(up_hbm.at[span], up_w.at[span], wsem.at[0, j]),
            pltpu.make_async_copy(down_hbm.at[span], down_w.at[span], wsem.at[1, j]),
        )

    for which in range(2):
        for j in range(full + (rem > 0)):
            weight_copies(j, TILE if j < full else rem)[which].start()
    in_landed.start()

    barrier = pltpu.get_barrier_semaphore()
    for d in range(1, n):
        pl.semaphore_signal(barrier, inc=1, device_id={"tensor": peer(d)}, device_id_type=MESH)

    @pl.when(has_next)
    def _():
        pl.semaphore_signal(barrier, inc=1, device_id={"pipe": sec - 1}, device_id_type=MESH)

    @pl.when(has_prev)
    def _():
        pl.semaphore_signal(barrier, inc=1, device_id={"pipe": sec + 1}, device_id_type=MESH)

    def stash_rows(q):
        tick, chunk = q // CHUNKS, q % CHUNKS
        values = stash[order[0, tick], chunk].astype(jnp.float32)
        factor = lax.rsqrt(jnp.mean(values * values, axis=-1, keepdims=True) + EPS)
        return factor, values * factor

    def spread(buf, send, recv, slot, d):
        return pltpu.make_async_remote_copy(
            src_ref=buf.at[slot, me],
            dst_ref=buf.at[slot, me],
            send_sem=send.at[slot, d - 1],
            recv_sem=recv.at[slot, d - 1],
            device_id={"tensor": peer(d)},
            device_id_type=MESH,
        )

    def part_copy(slot, d, span=slice(None)):
        return pltpu.make_async_remote_copy(
            src_ref=psend.at[slot, peer(d), :, span],
            dst_ref=precv.at[slot, d - 1, :, span],
            send_sem=p_send.at[slot, d - 1],
            recv_sem=p_recv.at[slot, d - 1],
            device_id={"tensor": peer(d)},
            device_id_type=MESH,
        )

    def pipe_copy(q):
        return pltpu.make_async_remote_copy(
            src_ref=moved_b.at[q],
            dst_ref=gin.at[q],
            send_sem=g_send.at[q],
            recv_sem=g_recv.at[q],
            device_id={"pipe": jnp.maximum(sec - 1, 0)},
            device_id_type=MESH,
        )

    def out_copy(q):
        return pltpu.make_async_copy(moved_b.at[q], out_hbm.at[q], o_sem.at[q])

    def act_copy(a, d):
        return spread(act, a_send, a_recv, a % HELD, d)

    def make_act(a):
        _, normed = stash_rows(a)
        act[a % HELD, me] = (normed * gain[...]).astype(jnp.bfloat16)

    def make_scaled(q):
        scaled[q % RING, me] = (grads[q % CHUNKS] * lscale[...]).astype(jnp.bfloat16)

    def scaled_copy(q, d):
        return spread(scaled, s_send, s_recv, q % RING, d)

    def finish(q):
        slot, chunk = q % RING, q % CHUNKS
        for d in range(1, n):
            part_copy(slot, d).wait_recv()
        total = psend[slot, me].astype(jnp.float32)
        for d in range(1, n):
            total += precv[slot, d - 1].astype(jnp.float32)
        factor, normed = stash_rows(q)
        back = total * gain[...]
        moved = grads[chunk] + factor * (back - normed * jnp.mean(back * normed, axis=-1, keepdims=True))
        moved_b[q] = moved.astype(jnp.bfloat16)

        @pl.when(has_next)
        def _():
            pipe_copy(q).start()

        out_copy(q).start()

    def next_grads(q):
        chunk, before = q % CHUNKS, q - CHUNKS

        @pl.when(is_last)
        def _():
            grads[chunk] = landed[before].astype(jnp.float32)

        @pl.when(has_prev)
        def _():
            pipe_copy(before).wait_recv()
            grads[chunk] = gin[before].astype(jnp.float32)

    in_stash.wait()
    in_grads.wait()
    for a in range(CHUNKS):
        make_act(a)
        if a == 0:
            waits = (n - 1) + has_next.astype(jnp.int32) + has_prev.astype(jnp.int32)
            pl.semaphore_wait(barrier, waits)
        for d in range(1, n):
            act_copy(a, d).start()
    for q in range(CHUNKS):
        make_scaled(q)
        for d in range(1, n):
            scaled_copy(q, d).start()
    in_landed.wait()

    tokens = n * rows

    def aligned(j):
        first = j * TILE
        return first if isinstance(j, int) else pl.multiple_of(first, TILE)

    ticks = steps // CHUNKS

    def send_act(a):
        @pl.when(a >= HELD)
        def _():
            for d in range(1, n):
                act_copy(a, d).wait_send()

        make_act(a)
        for d in range(1, n):
            act_copy(a, d).start()

    def send_next(q):
        for d in range(1, n):
            scaled_copy(q, d).wait_send()
        next_grads(q)
        make_scaled(q)
        for d in range(1, n):
            scaled_copy(q, d).start()

    def tick_of(tick, carry):
        head = tick * CHUNKS
        more = tick + 1 < ticks

        def arrive(which, j, size):
            @pl.when(tick == 0)
            def _():
                weight_copies(j, size)[which].wait()

        def hidden_tile(j, size):
            arrive(0, j, size)
            span = pl.ds(aligned(j), size)
            rows_of = act[pl.ds(head % HELD, CHUNKS)].reshape(CHUNKS * tokens, width)
            hidden = lax.dot_general(rows_of, up_w[span, :], NT, preferred_element_type=jnp.float32)
            factor_of[:, :, span] = gelu_slope(hidden).reshape(CHUNKS, tokens, size)

        for c in range(CHUNKS):
            for d in range(1, n):
                act_copy(head + c, d).wait_recv()
        pl.loop(0, full)(lambda j: hidden_tile(j, TILE))
        if rem:
            hidden_tile(full, rem)

        @pl.when(tick >= 1)
        def _():
            send_next(head + CHUNKS - 1)

        @pl.when(more)
        def _():
            send_act(head + CHUNKS)

        for c in range(CHUNKS):
            q = head + c
            for d in range(1, n):
                scaled_copy(q, d).wait_recv()

            def up_tile(j, size):
                if c == 0:
                    arrive(1, j, size)
                span = pl.ds(aligned(j), size)
                upstream = lax.dot_general(
                    scaled[c].reshape(tokens, width), down_w[span, :], NT, preferred_element_type=jnp.float32
                )
                slope[:, span] = (upstream * factor_of[c, :, span]).astype(jnp.bfloat16)

            pl.loop(0, full)(lambda j: up_tile(j, TILE))
            if rem:
                up_tile(full, rem)
            if c:
                finish(q - 1)

            @pl.when(tick >= 1)
            def _():
                for d in range(1, n):
                    part_copy(c, d).wait_send()

            def down_tile(j, size):
                span = pl.ds(aligned(j), size)
                part = jnp.dot(slope[...], up_w[:, span], preferred_element_type=jnp.float32)
                psend[c, :, :, span] = part.astype(jnp.bfloat16).reshape(n, rows, size)
                for d in range(1, n):
                    part_copy(c, d, span).start()

            pl.loop(0, wfull)(lambda j: down_tile(j, TILE))
            if wrem:
                down_tile(wfull, wrem)

            @pl.when(more)
            def _():
                if c:
                    send_next(q - 1 + CHUNKS)
                if c + 1 < CHUNKS:
                    send_act(q + 1 + CHUNKS)

        finish(head + CHUNKS - 1)
        return carry

    lax.fori_loop(0, ticks, tick_of, 0)

    for q in range(steps - CHUNKS, steps):
        @pl.when(has_prev)
        def _(q=q):
            pipe_copy(q).wait_recv()
            pltpu.make_async_copy(gin.at[q], pend_hbm.at[q - steps + CHUNKS], e_sem.at[q - steps + CHUNKS]).start()

    for q in range(steps):
        out_copy(q).wait()

        @pl.when(has_next)
        def _(q=q):
            pipe_copy(q).wait_send()

    for d in range(1, n):
        for slot in range(RING):
            scaled_copy(slot, d).wait_send()
            part_copy(slot, d).wait_send()
        for slot in range(min(HELD, steps)):
            act_copy(slot, d).wait_send()
    for c in range(CHUNKS):
        @pl.when(has_prev)
        def _(c=c):
            pltpu.make_async_copy(gin.at[steps - CHUNKS + c], pend_hbm.at[c], e_sem.at[c]).wait()


def shards(n, sections, up_weight, down_weight, norm_gain, layer_scale, stash, slot_order, received, arrivals):
    up_w, down_w = up_weight[0], down_weight[0]
    hid, width = up_w.shape
    _, ticks, tokens, _ = stash.shape
    half = GRID // 2
    lines = tokens // 4 // half
    rows = tokens // CHUNKS
    steps = ticks * CHUNKS
    landed = (
        arrivals.reshape(ticks, lines, half, 2, 2, width)
        .transpose(0, 1, 3, 2, 4, 5)
        .reshape(ticks, tokens, width)
    )
    bf = jnp.bfloat16
    hold = pl.BlockSpec(memory_space=pltpu.VMEM)
    far = pl.BlockSpec(memory_space=pl.ANY)
    dma = pltpu.SemaphoreType.DMA
    tile_count = hid // TILE + (hid % TILE > 0)
    out, pend = pl.pallas_call(
        functools.partial(kernel, n, sections, steps),
        out_shape=(
            jax.ShapeDtypeStruct((steps, rows, width), bf),
            jax.ShapeDtypeStruct((CHUNKS, rows, width), bf),
        ),
        in_specs=[pl.BlockSpec(memory_space=pltpu.SMEM), hold, hold, far, far, far, far, far],
        out_specs=(far, far),
        scratch_shapes=[
            pltpu.VMEM((hid, width), bf),
            pltpu.VMEM((hid, width), bf),
            pltpu.VMEM((ticks, CHUNKS, rows, width), bf),
            pltpu.VMEM((CHUNKS, rows, width), jnp.float32),
            pltpu.VMEM((steps - CHUNKS, rows, width), bf),
            pltpu.VMEM((HELD, n, rows, width), bf),
            pltpu.VMEM((RING, n, rows, width), bf),
            pltpu.VMEM((CHUNKS, n * rows, hid), jnp.float32),
            pltpu.VMEM((n * rows, hid), bf),
            pltpu.VMEM((RING, n, rows, width), bf),
            pltpu.VMEM((RING, n - 1, rows, width), bf),
            pltpu.VMEM((steps, rows, width), bf),
            pltpu.VMEM((steps, rows, width), bf),
            dma((2, tile_count)),
            dma((3,)),
            dma((HELD, n - 1)),
            dma((HELD, n - 1)),
            dma((RING, n - 1)),
            dma((RING, n - 1)),
            dma((RING, n - 1)),
            dma((RING, n - 1)),
            dma((steps,)),
            dma((steps,)),
            dma((steps,)),
            dma((CHUNKS,)),
        ],
        compiler_params=pltpu.CompilerParams(
            collective_id=0, has_side_effects=True, vmem_limit_bytes=67_043_328
        ),
    )(
        slot_order,
        norm_gain,
        layer_scale,
        up_w,
        down_w,
        stash.reshape(ticks, CHUNKS, rows, width),
        received.reshape(CHUNKS, rows, width),
        landed[: ticks - 1].reshape(steps - CHUNKS, rows, width),
    )
    is_last = lax.axis_index("pipe") == sections - 1
    pending = jnp.where(is_last, landed[ticks - 1], pend.reshape(tokens, width)).astype(jnp.float32)
    return out.reshape(1, ticks, tokens, width), pending[None]


def solution(mesh):
    return jax.shard_map(
        functools.partial(shards, mesh.shape["tensor"], mesh.shape["pipe"]),
        mesh=mesh,
        in_specs=(
            P("pipe", "tensor", None),
            P("pipe", "tensor", None),
            P("pipe", None),
            P("pipe", None),
            P("pipe", None, "tensor", None),
            P("pipe", None),
            P("pipe", "tensor", None),
            P(None, "tensor", None),
        ),
        out_specs=(P("pipe", None, "tensor", None), P("pipe", "tensor", None)),
        check_vma=False,
    )
```

profile of v0, /device:TPU:1, one launch (start us, length us, event | category | flops | bytes accessed | tf_op | source)
XLA Modules:
  0.0 203.7 jit_solution(11925681515953142390)
XLA Ops:
  0.6 3.6 %copy.12 = bf16[3,4,8,2,2,3200]{5,4,2,3,1,0:T(2,128)(2,1)S(1)} copy(bf16[3,4,8,2,2,3200]{5,2,4,3,1,0:T(8,128)(2,1)} %bitcast.19) | data formatting | bytes 4915200 | tf_op jit(solution)/shard_map/reshape | solution.py:319
  4.2 0.6 slice.11
  4.8 1.1 slice.10
  5.9 1.5 reshape.50.landed_hbm
  7.5 1.2 squeeze.11
  8.7 191.0 %shard_map.95 = (bf16[6,64,3200]{2,1,0:T(8,128)(2,1)}, bf16[2,64,3200]{2,1,0:T(8,128)(2,1)}) custom-call(s32[1,3]{1,0:T(1,128)} %order.1, f32[1,3200]{1,0:T(1,128)} %gain.1, f32[1,3200]{1,0:T(1,128)} %lscale.1, bf16[3200,3200]{1,0:T(8,128)(2,1)} %bitcast.14, bf16[3200,3200]{1,0:T(8,128)(2,1)} %bitcast.15, bf16[3,2,64,3200]{3,2,1,0:T(8,128)(2,1)} %bitcast.18, ...), custom_call_target="tpu_custom_call" | custom-call | tf_op jit(solution)/shard_map/pallas_call | solution.py:328
  199.7 0.0 copy-start
  199.7 2.6 %fusion = f32[1,128,3200]{2,1,0:T(8,128)} fusion(bf16[1,128,3200]{2,1,0:T(8,128)(2,1)} %squeeze.11, pred[]{:T(512)S(6)} %eq.3, bf16[1,128,3200]{2,1,0:T(8,128)(2,1)} %bitcast.22), kind=kLoop, calls=%fused_computation.2 | loop fusion | flops 819200 | bytes 3276801 | tf_op jit(solution)/shard_map/convert_element_type | solution.py:377
  202.3 0.0 copy-done
  202.3 1.4 copy.14
Async XLA Ops:
  199.7 2.6 %copy-start = (bf16[6,64,3200]{2,1,0:T(8,128)(2,1)S(1)}, bf16[6,64,3200]{2,1,0:T(8,128)(2,1)}, u32[]{:S(2)}) copy-start(bf16[6,64,3200]{2,1,0:T(8,128)(2,1)} %get-tuple-element.4) | copy-start | bytes 7372804
where the time goes:
time: 204 us
  Pallas kernels  191 us (94%)
  local copies, waits for them, and re-layouts  9.46 us (5%)
  other arithmetic  2.59 us (1%)
    pallas_call x1, Pallas kernels, shards(): pl.pallas_call(functools.partial(kernel, n, sections, steps), out_shape=(...  191 us

commit v1 on v0

--- a/solution.py
+++ b/solution.py
@@ -29,10 +29,10 @@
 
 
 def kernel(
-    n, sections, steps, order, gain, lscale, up_hbm, down_hbm, stash_hbm, received_hbm, landed_hbm,
+    n, sections, steps, order, gain, lscale, up_hbm, down_hbm, stash_hbm, received_hbm, arrivals_hbm,
     out_hbm, pend_hbm,
-    up_w, down_w, stash, grads, landed, act, scaled, factor_of, slope, psend, precv, gin, moved_b,
-    wsem, isem, a_send, a_recv, s_send, s_recv, p_send, p_recv, g_send, g_recv, o_sem, e_sem,
+    up_w, down_w, stash, grads, act, scaled, factor_of, slope, psend, precv, gin, moved_b,
+    wsem, isem, l_sem, a_send, a_recv, s_send, s_recv, p_send, p_recv, g_send, g_recv, o_sem, e_sem,
 ):
     hid, width = up_w.shape
     rows = grads.shape[1]
@@ -43,21 +43,24 @@
     is_last = sec == sections - 1
     full, rem = tiles_of(hid)
     wfull, wrem = tiles_of(width)
+    ticks = steps // CHUNKS
+    tokens = n * rows
+    piece = rows // 4
 
     def peer(d):
         return lax.rem(me + d, n)
 
     in_stash = pltpu.make_async_copy(stash_hbm, stash, isem.at[0])
     in_grads = pltpu.make_async_copy(received_hbm, grads, isem.at[1])
-    in_landed = pltpu.make_async_copy(landed_hbm, landed, isem.at[2])
     in_stash.start()
     in_grads.start()
 
+    def aligned(j):
+        first = j * TILE
+        return first if isinstance(j, int) else pl.multiple_of(first, TILE)
+
     def weight_copies(j, size):
-        first = j * TILE
-        if not isinstance(j, int):
-            first = pl.multiple_of(first, TILE)
-        span = pl.ds(first, size)
+        span = pl.ds(aligned(j), size)
         return (
             pltpu.make_async_copy(up_hbm.at[span], up_w.at[span], wsem.at[0, j]),
             pltpu.make_async_copy(down_hbm.at[span], down_w.at[span], wsem.at[1, j]),
@@ -66,7 +69,23 @@
     for which in range(2):
         for j in range(full + (rem > 0)):
             weight_copies(j, TILE if j < full else rem)[which].start()
-    in_landed.start()
+
+    def landing(q, k):
+        if isinstance(q, int):
+            first = (q % CHUNKS) * piece
+        else:
+            first = pl.multiple_of(lax.rem(q, CHUNKS) * piece, piece)
+        return pltpu.make_async_copy(
+            arrivals_hbm.at[q // CHUNKS, pl.ds(first, piece), pl.ds(k * width, width)],
+            gin.at[q, pl.ds(k * piece, piece)],
+            l_sem.at[q, k],
+        )
+
+    @pl.when(is_last)
+    def _():
+        for q in range(steps):
+            for k in range(4):
+                landing(q, k).start()
 
     barrier = pltpu.get_barrier_semaphore()
     for d in range(1, n):
@@ -122,23 +141,32 @@
     def act_copy(a, d):
         return spread(act, a_send, a_recv, a % HELD, d)
 
+    def scaled_copy(q, d):
+        return spread(scaled, s_send, s_recv, q % RING, d)
+
     def make_act(a):
         _, normed = stash_rows(a)
         act[a % HELD, me] = (normed * gain[...]).astype(jnp.bfloat16)
 
+    def send_act(a):
+        @pl.when(a >= HELD)
+        def _():
+            for d in range(1, n):
+                act_copy(a, d).wait_send()
+
+        make_act(a)
+        for d in range(1, n):
+            act_copy(a, d).start()
+
     def make_scaled(q):
         scaled[q % RING, me] = (grads[q % CHUNKS] * lscale[...]).astype(jnp.bfloat16)
 
-    def scaled_copy(q, d):
-        return spread(scaled, s_send, s_recv, q % RING, d)
-
-    def finish(q):
-        slot, chunk = q % RING, q % CHUNKS
-        for d in range(1, n):
-            part_copy(slot, d).wait_recv()
-        total = psend[slot, me].astype(jnp.float32)
-        for d in range(1, n):
-            total += precv[slot, d - 1].astype(jnp.float32)
+    def finish(q, chunk):
+        for d in range(1, n):
+            part_copy(chunk, d).wait_recv()
+        total = psend[chunk, me].astype(jnp.float32)
+        for d in range(1, n):
+            total += precv[chunk, d - 1].astype(jnp.float32)
         factor, normed = stash_rows(q)
         back = total * gain[...]
         moved = grads[chunk] + factor * (back - normed * jnp.mean(back * normed, axis=-1, keepdims=True))
@@ -150,20 +178,37 @@
 
         out_copy(q).start()
 
-    def next_grads(q):
-        chunk, before = q % CHUNKS, q - CHUNKS
-
+    def take_landed(q, chunk):
+        for k in range(4):
+            landing(q, k).wait()
+        token = lax.broadcasted_iota(jnp.int32, (rows, rows), 0)
+        source = lax.broadcasted_iota(jnp.int32, (rows, rows), 1)
+        line, within = token // (2 * GRID), token % (2 * GRID)
+        block = 2 * (within // GRID) + within % 2
+        wanted = block * piece + line * (GRID // 2) + (within % GRID) // 2
+        shuffle = jnp.where(source == wanted, 1.0, 0.0).astype(jnp.bfloat16)
+        grads[chunk] = jnp.dot(shuffle, gin[q], preferred_element_type=jnp.float32)
+
+    def next_grads(before, chunk):
         @pl.when(is_last)
         def _():
-            grads[chunk] = landed[before].astype(jnp.float32)
+            take_landed(before, chunk)
 
         @pl.when(has_prev)
         def _():
             pipe_copy(before).wait_recv()
             grads[chunk] = gin[before].astype(jnp.float32)
 
+    def send_next(before, chunk):
+        q = before + CHUNKS
+        for d in range(1, n):
+            scaled_copy(q, d).wait_send()
+        next_grads(before, chunk)
+        make_scaled(q)
+        for d in range(1, n):
+            scaled_copy(q, d).start()
+
     in_stash.wait()
-    in_grads.wait()
     for a in range(CHUNKS):
         make_act(a)
         if a == 0:
@@ -171,34 +216,8 @@
             pl.semaphore_wait(barrier, waits)
         for d in range(1, n):
             act_copy(a, d).start()
+    in_grads.wait()
     for q in range(CHUNKS):
-        make_scaled(q)
-        for d in range(1, n):
-            scaled_copy(q, d).start()
-    in_landed.wait()
-
-    tokens = n * rows
-
-    def aligned(j):
-        first = j * TILE
-        return first if isinstance(j, int) else pl.multiple_of(first, TILE)
-
-    ticks = steps // CHUNKS
-
-    def send_act(a):
-        @pl.when(a >= HELD)
-        def _():
-            for d in range(1, n):
-                act_copy(a, d).wait_send()
-
-        make_act(a)
-        for d in range(1, n):
-            act_copy(a, d).start()
-
-    def send_next(q):
-        for d in range(1, n):
-            scaled_copy(q, d).wait_send()
-        next_grads(q)
         make_scaled(q)
         for d in range(1, n):
             scaled_copy(q, d).start()
@@ -211,6 +230,11 @@
             @pl.when(tick == 0)
             def _():
                 weight_copies(j, size)[which].wait()
+
+        @pl.when(more)
+        def _():
+            for c in range(CHUNKS - 1):
+                send_act(head + CHUNKS + c)
 
         def hidden_tile(j, size):
             arrive(0, j, size)
@@ -225,14 +249,6 @@
         pl.loop(0, full)(lambda j: hidden_tile(j, TILE))
         if rem:
             hidden_tile(full, rem)
-
-        @pl.when(tick >= 1)
-        def _():
-            send_next(head + CHUNKS - 1)
-
-        @pl.when(more)
-        def _():
-            send_act(head + CHUNKS)
 
         for c in range(CHUNKS):
             q = head + c
@@ -251,8 +267,6 @@
             pl.loop(0, full)(lambda j: up_tile(j, TILE))
             if rem:
                 up_tile(full, rem)
-            if c:
-                finish(q - 1)
 
             @pl.when(tick >= 1)
             def _():
@@ -270,23 +284,41 @@
             if wrem:
                 down_tile(wfull, wrem)
 
+        @pl.when(more)
+        def _():
+            send_act(head + 2 * CHUNKS - 1)
+
+        for c in range(CHUNKS):
+            finish(head + c, c)
+
             @pl.when(more)
             def _():
-                if c:
-                    send_next(q - 1 + CHUNKS)
-                if c + 1 < CHUNKS:
-                    send_act(q + 1 + CHUNKS)
-
-        finish(head + CHUNKS - 1)
+                send_next(head + c, c)
+
         return carry
 
     lax.fori_loop(0, ticks, tick_of, 0)
 
-    for q in range(steps - CHUNKS, steps):
+    for d in range(1, n):
+        for slot in range(RING):
+            scaled_copy(slot, d).wait_send()
+
+    def end_copy(c, src):
+        return pltpu.make_async_copy(src, pend_hbm.at[c], e_sem.at[c])
+
+    for c in range(CHUNKS):
+        q = steps - CHUNKS + c
+
+        @pl.when(is_last)
+        def _(c=c, q=q):
+            take_landed(q, c)
+            scaled[c, me] = grads[c].astype(jnp.bfloat16)
+            end_copy(c, scaled.at[c, me]).start()
+
         @pl.when(has_prev)
-        def _(q=q):
+        def _(c=c, q=q):
             pipe_copy(q).wait_recv()
-            pltpu.make_async_copy(gin.at[q], pend_hbm.at[q - steps + CHUNKS], e_sem.at[q - steps + CHUNKS]).start()
+            end_copy(c, gin.at[q]).start()
 
     for q in range(steps):
         out_copy(q).wait()
@@ -297,29 +329,19 @@
 
     for d in range(1, n):
         for slot in range(RING):
-            scaled_copy(slot, d).wait_send()
             part_copy(slot, d).wait_send()
         for slot in range(min(HELD, steps)):
             act_copy(slot, d).wait_send()
     for c in range(CHUNKS):
-        @pl.when(has_prev)
-        def _(c=c):
-            pltpu.make_async_copy(gin.at[steps - CHUNKS + c], pend_hbm.at[c], e_sem.at[c]).wait()
+        end_copy(c, gin.at[steps - CHUNKS + c]).wait()
 
 
 def shards(n, sections, up_weight, down_weight, norm_gain, layer_scale, stash, slot_order, received, arrivals):
     up_w, down_w = up_weight[0], down_weight[0]
     hid, width = up_w.shape
     _, ticks, tokens, _ = stash.shape
-    half = GRID // 2
-    lines = tokens // 4 // half
     rows = tokens // CHUNKS
     steps = ticks * CHUNKS
-    landed = (
-        arrivals.reshape(ticks, lines, half, 2, 2, width)
-        .transpose(0, 1, 3, 2, 4, 5)
-        .reshape(ticks, tokens, width)
-    )
     bf = jnp.bfloat16
     hold = pl.BlockSpec(memory_space=pltpu.VMEM)
     far = pl.BlockSpec(memory_space=pl.ANY)
@@ -338,7 +360,6 @@
             pltpu.VMEM((hid, width), bf),
             pltpu.VMEM((ticks, CHUNKS, rows, width), bf),
             pltpu.VMEM((CHUNKS, rows, width), jnp.float32),
-            pltpu.VMEM((steps - CHUNKS, rows, width), bf),
             pltpu.VMEM((HELD, n, rows, width), bf),
             pltpu.VMEM((RING, n, rows, width), bf),
             pltpu.VMEM((CHUNKS, n * rows, hid), jnp.float32),
@@ -348,7 +369,8 @@
             pltpu.VMEM((steps, rows, width), bf),
             pltpu.VMEM((steps, rows, width), bf),
             dma((2, tile_count)),
-            dma((3,)),
+            dma((2,)),
+            dma((steps, 4)),
             dma((HELD, n - 1)),
             dma((HELD, n - 1)),
             dma((RING, n - 1)),
@@ -371,10 +393,9 @@
         down_w,
         stash.reshape(ticks, CHUNKS, rows, width),
         received.reshape(CHUNKS, rows, width),
-        landed[: ticks - 1].reshape(steps - CHUNKS, rows, width),
+        arrivals,
     )
-    is_last = lax.axis_index("pipe") == sections - 1
-    pending = jnp.where(is_last, landed[ticks - 1], pend.reshape(tokens, width)).astype(jnp.float32)
+    pending = pend.reshape(tokens, width).astype(jnp.float32)
     return out.reshape(1, ticks, tokens, width), pending[None]
 
 

time: 204 us -> 192 us (0.941)
  local copies, waits for them, and re-layouts: 9.46 us -> 1.44 us
  Pallas kernels: 191 us -> 187 us
    reshape x2 -> x0, local copies, waits for them, and re-layouts: 5.13 us -> none  [the longest x1 3.59 us: shards(): arrivals.reshape(ticks, lines, half, 2, 2, width)]
    pallas_call x1, Pallas kernels: 191 us -> 187 us  [shards(): pl.pallas_call(functools.partial(kernel, n, sections, steps), out_shape=(...]
where the time goes in v1:
time: 192 us; the launch traced here: 191 us
  Pallas kernels  187 us (97%)
  other arithmetic  2.57 us (1%)
    pallas_call x1, Pallas kernels, shards(): pl.pallas_call(functools.partial(kernel, n, sections, steps), out_shape=(...  187 us

profile of v1, /device:TPU:1, one launch (start us, length us, event | category | flops | bytes accessed | tf_op | source)
XLA Modules:
  0.0 191.3 jit_solution(17400242871056290627)
XLA Ops:
  0.6 186.6 %shard_map.95 = (bf16[6,64,3200]{2,1,0:T(8,128)(2,1)}, bf16[2,64,3200]{2,1,0:T(8,128)(2,1)}) custom-call(s32[1,3]{1,0:T(1,128)} %order.1, f32[1,3200]{1,0:T(1,128)} %gain.1, f32[1,3200]{1,0:T(1,128)} %lscale.1, bf16[3200,3200]{1,0:T(8,128)(2,1)} %bitcast.9, bf16[3200,3200]{1,0:T(8,128)(2,1)} %bitcast.10, bf16[3,2,64,3200]{3,2,1,0:T(8,128)(2,1)} %bitcast.12, ...), custom_call_target="tpu_custom_call" | custom-call | tf_op jit(solution)/shard_map/pallas_call | solution.py:350
  187.2 0.0 copy-start
  187.3 2.6 %bitcast_convert_fusion = f32[1,128,3200]{2,1,0:T(8,128)} fusion(bf16[1,128,3200]{2,1,0:T(8,128)(2,1)} %bitcast.14), kind=kLoop, calls=%fused_computation | loop fusion | flops 409600 | bytes 2457600 | tf_op jit(solution)/shard_map/convert_element_type | solution.py:398
  189.8 0.0 copy-done
  189.8 1.4 copy.11
Async XLA Ops:
  187.2 2.6 %copy-start = (bf16[6,64,3200]{2,1,0:T(8,128)(2,1)S(1)}, bf16[6,64,3200]{2,1,0:T(8,128)(2,1)}, u32[]{:S(2)}) copy-start(bf16[6,64,3200]{2,1,0:T(8,128)(2,1)} %get-tuple-element.4) | copy-start | bytes 7372804

commit v2 on v1

v2 whole, which is shorter than its diff:
```python
import functools

import jax
import jax.numpy as jnp
from jax import lax
from jax.experimental import pallas as pl
from jax.experimental.pallas import tpu as pltpu
from jax.sharding import PartitionSpec as P

GRID = 16
EPS = 1e-06
CHUNKS = 2
HELD = 2 * CHUNKS
TILE = 512
BLOCK = 128
STAGES = 3
PIECE = 16
MESH = pl.DeviceIdType.MESH
NT = (((1,), (1,)), ((), ()))


def gelu_slope(hidden):
    return (
        0.5 * (1.0 + lax.erf(hidden * 0.7071067811865476))
        + hidden * jnp.exp(-0.5 * hidden * hidden) * 0.3989422804014327
    )


def tiles_of(size):
    return size // TILE, size % TILE


def kernel(
    n, sections, steps, order, gain, lscale, up_hbm, down_hbm, stash_hbm, received_hbm, arrivals_hbm,
    out_hbm, pend_hbm,
    up_w, down_t, stash0, stash1, grads, act, scaled, factor_of, slope, psend, precv, gin, moved_b,
    wsem, tsem, isem, l_sem, a_send, a_recv, s_send, s_recv, p_send, p_recv, g_send, g_recv, o_sem, e_sem,
):
    hid, width = up_w.shape
    rows = grads.shape[1]
    me = lax.axis_index("tensor")
    sec = lax.axis_index("pipe")
    has_next = sec > 0
    has_prev = sec < sections - 1
    is_last = sec == sections - 1
    full, rem = tiles_of(hid)
    wfull, wrem = tiles_of(width)
    ticks = steps // CHUNKS
    tokens = n * rows
    quarter = rows // 4
    stash = (stash0, stash1)
    whole = ((0, rows),)
    pieces = tuple((first, PIECE) for first in range(0, rows, PIECE))

    def pieces_of(chunk):
        return pieces if chunk == CHUNKS - 1 else whole

    def peer(d):
        return lax.rem(me + d, n)

    def rows_at(device, first, size):
        return pl.ds(pl.multiple_of(device * rows + first, PIECE if first else size), size)

    def in_stash(c):
        return pltpu.make_async_copy(stash_hbm.at[:, c], stash[c], isem.at[0, c])

    def in_grads(c):
        return pltpu.make_async_copy(received_hbm.at[c], grads.at[c], isem.at[1, c])

    for c in range(CHUNKS):
        in_stash(c).start()
    for c in range(CHUNKS):
        in_grads(c).start()

    def aligned(j, size):
        first = j * size
        return first if isinstance(j, int) else pl.multiple_of(first, size)

    def up_copy(j, size):
        span = pl.ds(aligned(j, TILE), size)
        return pltpu.make_async_copy(up_hbm.at[span], up_w.at[span], wsem.at[j])

    blocks, left = hid // BLOCK, hid % BLOCK

    def stage_copy(g, size):
        slot = g % STAGES if isinstance(g, int) else lax.rem(g, STAGES)
        return pltpu.make_async_copy(
            down_hbm.at[pl.ds(aligned(g, BLOCK), size)], psend.at[slot, pl.ds(0, size)], tsem.at[slot]
        )

    def load_weights():
        for g in range(STAGES):
            stage_copy(g, BLOCK).start()
        for j in range(full + (rem > 0)):
            up_copy(j, TILE if j < full else rem).start()

    def turn(g):
        stage_copy(g, BLOCK).wait()
        down_t[:, pl.ds(aligned(g, BLOCK), BLOCK)] = psend[lax.rem(g, STAGES), :BLOCK].T

        @pl.when(g + STAGES < blocks)
        def _():
            stage_copy(g + STAGES, BLOCK).start()

    def turn_down():
        pl.loop(0, blocks)(turn)
        if left:
            stage_copy(blocks, left).start()
            stage_copy(blocks, left).wait()
            down_t[:, pl.ds(blocks * BLOCK, left)] = psend[blocks % STAGES, :left].T

    def landing(q, k):
        if isinstance(q, int):
            first = (q % CHUNKS) * quarter
        else:
            first = pl.multiple_of(lax.rem(q, CHUNKS) * quarter, quarter)
        return pltpu.make_async_copy(
            arrivals_hbm.at[q // CHUNKS, pl.ds(first, quarter), pl.ds(k * width, width)],
            gin.at[q, pl.ds(k * quarter, quarter)],
            l_sem.at[q, k],
        )

    barrier = pltpu.get_barrier_semaphore()
    for d in range(1, n):
        pl.semaphore_signal(barrier, inc=1, device_id={"tensor": peer(d)}, device_id_type=MESH)

    @pl.when(has_next)
    def _():
        pl.semaphore_signal(barrier, inc=1, device_id={"pipe": sec - 1}, device_id_type=MESH)

    @pl.when(has_prev)
    def _():
        pl.semaphore_signal(barrier, inc=1, device_id={"pipe": sec + 1}, device_id_type=MESH)

    def stash_rows(tick, chunk, first, size):
        values = stash[chunk][order[0, tick], pl.ds(first, size)].astype(jnp.float32)
        factor = lax.rsqrt(jnp.mean(values * values, axis=-1, keepdims=True) + EPS)
        return factor, values * factor

    def spread(buf, send, recv, slot, d):
        return pltpu.make_async_remote_copy(
            src_ref=buf.at[slot, me],
            dst_ref=buf.at[slot, me],
            send_sem=send.at[slot, d - 1],
            recv_sem=recv.at[slot, d - 1],
            device_id={"tensor": peer(d)},
            device_id_type=MESH,
        )

    def part_copy(slot, d, first, size, i, span=slice(None)):
        return pltpu.make_async_remote_copy(
            src_ref=psend.at[slot, rows_at(peer(d), first, size), span],
            dst_ref=precv.at[slot, d - 1, pl.ds(first, size), span],
            send_sem=p_send.at[slot, d - 1, i],
            recv_sem=p_recv.at[slot, d - 1, i],
            device_id={"tensor": peer(d)},
            device_id_type=MESH,
        )

    def pipe_copy(q, first, size, i, ends):
        target = pend_hbm.at[q - steps + CHUNKS] if ends else gin.at[q]
        return pltpu.make_async_remote_copy(
            src_ref=moved_b.at[q, pl.ds(first, size)],
            dst_ref=target.at[pl.ds(first, size)],
            send_sem=g_send.at[q, i],
            recv_sem=g_recv.at[q, i],
            device_id={"pipe": jnp.maximum(sec - 1, 0)},
            device_id_type=MESH,
        )

    def out_copy(q, first, size, i):
        span = pl.ds(first, size)
        return pltpu.make_async_copy(moved_b.at[q, span], out_hbm.at[q, span], o_sem.at[q, i])

    def act_copy(tick, chunk, d):
        return spread(act, a_send, a_recv, lax.rem(tick, HELD // CHUNKS) * CHUNKS + chunk, d)

    def scaled_copy(chunk, d):
        return spread(scaled, s_send, s_recv, chunk, d)

    def send_act(tick, chunk, reused=True):
        if reused:
            @pl.when(tick >= HELD // CHUNKS)
            def _():
                for d in range(1, n):
                    act_copy(tick, chunk, d).wait_send()

        _, normed = stash_rows(tick, chunk, 0, rows)
        act[lax.rem(tick, HELD // CHUNKS) * CHUNKS + chunk, me] = (normed * gain[...]).astype(jnp.bfloat16)
        for d in range(1, n):
            act_copy(tick, chunk, d).start()

    def send_scaled(chunk):
        scaled[chunk, me] = (grads[chunk] * lscale[...]).astype(jnp.bfloat16)
        for d in range(1, n):
            scaled_copy(chunk, d).start()

    def finish(tick, chunk, more):
        q = tick * CHUNKS + chunk
        for i, (first, size) in enumerate(pieces_of(chunk)):
            span = pl.ds(first, size)
            for d in range(1, n):
                part_copy(chunk, d, first, size, i).wait_recv()
            total = psend[chunk, rows_at(me, first, size), :].astype(jnp.float32)
            for d in range(1, n):
                total += precv[chunk, d - 1, span].astype(jnp.float32)
            factor, normed = stash_rows(tick, chunk, first, size)
            back = total * gain[...]
            moved = grads[chunk, span] + factor * (back - normed * jnp.mean(back * normed, axis=-1, keepdims=True))
            moved_b[q, span] = moved.astype(jnp.bfloat16)

            @pl.when(has_next & more)
            def _():
                pipe_copy(q, first, size, i, False).start()

            @pl.when(has_next & jnp.logical_not(more))
            def _():
                pipe_copy(steps - CHUNKS + chunk, first, size, i, True).start()

            out_copy(q, first, size, i).start()

    def take_landed(q, chunk):
        for k in range(4):
            landing(q, k).wait()
        token = lax.broadcasted_iota(jnp.int32, (rows, rows), 0)
        source = lax.broadcasted_iota(jnp.int32, (rows, rows), 1)
        line, within = token // (2 * GRID), token % (2 * GRID)
        block = 2 * (within // GRID) + within % 2
        wanted = block * quarter + line * (GRID // 2) + (within % GRID) // 2
        shuffle = jnp.where(source == wanted, 1.0, 0.0).astype(jnp.bfloat16)
        grads[chunk] = jnp.dot(shuffle, gin[q], preferred_element_type=jnp.float32)

    def send_next(tick, chunk):
        before = tick * CHUNKS + chunk
        for d in range(1, n):
            scaled_copy(chunk, d).wait_send()

        @pl.when(is_last)
        def _():
            take_landed(before, chunk)

        @pl.when(has_prev)
        def _():
            for i, (first, size) in enumerate(pieces_of(chunk)):
                pipe_copy(before, first, size, i, False).wait_recv()
            grads[chunk] = gin[before].astype(jnp.float32)

        send_scaled(chunk)

    for c in range(CHUNKS):
        in_stash(c).wait()
        if c == 0:
            waits = (n - 1) + has_next.astype(jnp.int32) + has_prev.astype(jnp.int32)
            pl.semaphore_wait(barrier, waits)
        send_act(0, c, reused=False)
    for c in range(CHUNKS):
        in_grads(c).wait()
    load_weights()
    for c in range(CHUNKS):
        send_scaled(c)
    for c in range(CHUNKS - 1):
        send_act(1, c, reused=False)

    @pl.when(is_last)
    def _():
        for q in range(steps):
            for k in range(4):
                landing(q, k).start()

    turn_down()
    for j in range(full + (rem > 0)):
        up_copy(j, TILE if j < full else rem).wait()

    def tick_of(tick, carry):
        more = tick + 1 < ticks

        def hidden_tile(j, size):
            span = pl.ds(aligned(j, TILE), size)
            held = act[pl.ds(lax.rem(tick, HELD // CHUNKS) * CHUNKS, CHUNKS)].reshape(CHUNKS * tokens, width)
            hidden = lax.dot_general(held, up_w[span, :], NT, preferred_element_type=jnp.float32)
            factor_of[:, :, span] = gelu_slope(hidden).reshape(CHUNKS, tokens, size)

        for c in range(CHUNKS):
            for d in range(1, n):
                act_copy(tick, c, d).wait_recv()
        pl.loop(0, full)(lambda j: hidden_tile(j, TILE))
        if rem:
            hidden_tile(full, rem)

        for c in range(CHUNKS):
            for d in range(1, n):
                scaled_copy(c, d).wait_recv()

            def up_tile(j, size):
                span = pl.ds(aligned(j, TILE), size)
                upstream = jnp.dot(
                    scaled[c].reshape(tokens, width), down_t[:, span], preferred_element_type=jnp.float32
                )
                slope[:, span] = (upstream * factor_of[c, :, span]).astype(jnp.bfloat16)

            pl.loop(0, full)(lambda j: up_tile(j, TILE))
            if rem:
                up_tile(full, rem)

            @pl.when(tick >= 1)
            def _():
                for i, (first, size) in enumerate(pieces_of(c)):
                    for d in range(1, n):
                        part_copy(c, d, first, size, i).wait_send()

            def down_tile(j, size):
                span = pl.ds(aligned(j, TILE), size)
                part = jnp.dot(slope[...], up_w[:, span], preferred_element_type=jnp.float32)
                psend[c, :, span] = part.astype(jnp.bfloat16)
                if c < CHUNKS - 1:
                    for d in range(1, n):
                        part_copy(c, d, 0, rows, 0, span).start()

            pl.loop(0, wfull)(lambda j: down_tile(j, TILE))
            if wrem:
                down_tile(wfull, wrem)
            if c == CHUNKS - 1:
                for i, (first, size) in enumerate(pieces_of(c)):
                    for d in range(1, n):
                        part_copy(c, d, first, size, i).start()

        @pl.when(more)
        def _():
            send_act(tick + 1, CHUNKS - 1)

        for c in range(CHUNKS):
            finish(tick, c, more)

            @pl.when(more)
            def _():
                send_next(tick, c)

        @pl.when(tick + 2 < ticks)
        def _():
            for c in range(CHUNKS - 1):
                send_act(tick + 2, c)

        return carry

    lax.fori_loop(0, ticks, tick_of, 0)

    for d in range(1, n):
        for c in range(CHUNKS):
            scaled_copy(c, d).wait_send()

    def end_copy(c):
        return pltpu.make_async_copy(scaled.at[c, me], pend_hbm.at[c], e_sem.at[c])

    @pl.when(is_last)
    def _():
        for c in range(CHUNKS):
            take_landed(steps - CHUNKS + c, c)
            scaled[c, me] = grads[c].astype(jnp.bfloat16)
            end_copy(c).start()
        for c in range(CHUNKS):
            end_copy(c).wait()

    @pl.when(has_prev)
    def _():
        for c in range(CHUNKS):
            for i, (first, size) in enumerate(pieces_of(c)):
                pipe_copy(steps - CHUNKS + c, first, size, i, True).wait_recv()

    for q in range(steps):
        for i, (first, size) in enumerate(pieces_of(q % CHUNKS)):
            out_copy(q, first, size, i).wait()

            @pl.when(has_next)
            def _():
                pipe_copy(q, first, size, i, q >= steps - CHUNKS).wait_send()

    for d in range(1, n):
        for c in range(CHUNKS):
            for i, (first, size) in enumerate(pieces_of(c)):
                part_copy(c, d, first, size, i).wait_send()
        for slot in range(min(HELD, steps)):
            act_copy(slot // CHUNKS, slot % CHUNKS, d).wait_send()


def shards(n, sections, up_weight, down_weight, norm_gain, layer_scale, stash, slot_order, received, arrivals):
    up_w, down_w = up_weight[0], down_weight[0]
    hid, width = up_w.shape
    _, ticks, tokens, _ = stash.shape
    rows = tokens // CHUNKS
    steps = ticks * CHUNKS
    bf = jnp.bfloat16
    hold = pl.BlockSpec(memory_space=pltpu.VMEM)
    far = pl.BlockSpec(memory_space=pl.ANY)
    dma = pltpu.SemaphoreType.DMA
    tile_count = hid // TILE + (hid % TILE > 0)
    out, pend = pl.pallas_call(
        functools.partial(kernel, n, sections, steps),
        out_shape=(
            jax.ShapeDtypeStruct((steps, rows, width), bf),
            jax.ShapeDtypeStruct((CHUNKS, rows, width), bf),
        ),
        in_specs=[pl.BlockSpec(memory_space=pltpu.SMEM), hold, hold, far, far, far, far, far],
        out_specs=(far, far),
        scratch_shapes=[
            pltpu.VMEM((hid, width), bf),
            pltpu.VMEM((width, hid), bf),
            pltpu.VMEM((ticks, rows, width), bf),
            pltpu.VMEM((ticks, rows, width), bf),
            pltpu.VMEM((CHUNKS, rows, width), jnp.float32),
            pltpu.VMEM((HELD, n, rows, width), bf),
            pltpu.VMEM((CHUNKS, n, rows, width), bf),
            pltpu.VMEM((CHUNKS, n * rows, hid), jnp.float32),
            pltpu.VMEM((n * rows, hid), bf),
            pltpu.VMEM((STAGES, n * rows, width), bf),
            pltpu.VMEM((CHUNKS, n - 1, rows, width), bf),
            pltpu.VMEM((steps, rows, width), bf),
            pltpu.VMEM((steps, rows, width), bf),
            dma((tile_count,)),
            dma((STAGES,)),
            dma((2, CHUNKS)),
            dma((steps, 4)),
            dma((HELD, n - 1)),
            dma((HELD, n - 1)),
            dma((CHUNKS, n - 1)),
            dma((CHUNKS, n - 1)),
            dma((CHUNKS, n - 1, rows // PIECE)),
            dma((CHUNKS, n - 1, rows // PIECE)),
            dma((steps, rows // PIECE)),
            dma((steps, rows // PIECE)),
            dma((steps, rows // PIECE)),
            dma((CHUNKS,)),
        ],
        compiler_params=pltpu.CompilerParams(
            collective_id=0, has_side_effects=True, vmem_limit_bytes=67_043_328
        ),
    )(
        slot_order,
        norm_gain,
        layer_scale,
        up_w,
        down_w,
        stash.reshape(ticks, CHUNKS, rows, width),
        received.reshape(CHUNKS, rows, width),
        arrivals,
    )
    pending = pend.reshape(tokens, width).astype(jnp.float32)
    return out.reshape(1, ticks, tokens, width), pending[None]


def solution(mesh):
    return jax.shard_map(
        functools.partial(shards, mesh.shape["tensor"], mesh.shape["pipe"]),
        mesh=mesh,
        in_specs=(
            P("pipe", "tensor", None),
            P("pipe", "tensor", None),
            P("pipe", None),
            P("pipe", None),
            P("pipe", None, "tensor", None),
            P("pipe", None),
            P("pipe", "tensor", None),
            P(None, "tensor", None),
        ),
        out_specs=(P("pipe", None, "tensor", None), P("pipe", "tensor", None)),
        check_vma=False,
    )
```

time: 192 us -> 175 us (0.911)
  Pallas kernels: 187 us -> 170 us
    pallas_call x1, Pallas kernels: 187 us -> 170 us  [shards(): pl.pallas_call(functools.partial(kernel, n, sections, steps), out_shape=(...]
where the time goes in v2:
time: 175 us
  Pallas kernels  170 us (97%)
  other arithmetic  2.57 us (1%)
    pallas_call x1, Pallas kernels, shards(): pl.pallas_call(functools.partial(kernel, n, sections, steps), out_shape=(...  170 us

profile of v2, /device:TPU:1, one launch (start us, length us, event | category | flops | bytes accessed | tf_op | source)
XLA Modules:
  0.0 174.7 jit_solution(6511449702723511480)
XLA Ops:
  0.6 170.0 %shard_map.95 = (bf16[6,64,3200]{2,1,0:T(8,128)(2,1)}, bf16[2,64,3200]{2,1,0:T(8,128)(2,1)}) custom-call(s32[1,3]{1,0:T(1,128)} %order.1, f32[1,3200]{1,0:T(1,128)} %gain.1, f32[1,3200]{1,0:T(1,128)} %lscale.1, bf16[3200,3200]{1,0:T(8,128)(2,1)} %bitcast.9, bf16[3200,3200]{1,0:T(8,128)(2,1)} %bitcast.10, bf16[3,2,64,3200]{3,2,1,0:T(8,128)(2,1)} %bitcast.12, ...), custom_call_target="tpu_custom_call" | custom-call | tf_op jit(solution)/shard_map/pallas_call | solution.py:396
  170.6 0.0 copy-start
  170.6 2.6 %bitcast_convert_fusion = f32[1,128,3200]{2,1,0:T(8,128)} fusion(bf16[1,128,3200]{2,1,0:T(8,128)(2,1)} %bitcast.14), kind=kLoop, calls=%fused_computation | loop fusion | flops 409600 | bytes 2457600 | tf_op jit(solution)/shard_map/convert_element_type | solution.py:446
  173.2 0.0 copy-done
  173.2 1.4 copy.11
Async XLA Ops:
  170.6 2.6 %copy-start = (bf16[6,64,3200]{2,1,0:T(8,128)(2,1)S(1)}, bf16[6,64,3200]{2,1,0:T(8,128)(2,1)}, u32[]{:S(2)}) copy-start(bf16[6,64,3200]{2,1,0:T(8,128)(2,1)} %get-tuple-element.4) | copy-start | bytes 7372804

commit v3 on v2

--- a/solution.py
+++ b/solution.py
@@ -32,9 +32,9 @@
 
 def kernel(
     n, sections, steps, order, gain, lscale, up_hbm, down_hbm, stash_hbm, received_hbm, arrivals_hbm,
-    out_hbm, pend_hbm,
-    up_w, down_t, stash0, stash1, grads, act, scaled, factor_of, slope, psend, precv, gin, moved_b,
-    wsem, tsem, isem, l_sem, a_send, a_recv, s_send, s_recv, p_send, p_recv, g_send, g_recv, o_sem, e_sem,
+    moved_b, pend_hbm,
+    up_w, down_t, stash0, stash1, grads, act, scaled, factor_of, slope, psend, precv, gin,
+    wsem, tsem, isem, l_sem, a_send, a_recv, s_send, s_recv, p_send, p_recv, g_send, g_recv, e_sem,
 ):
     hid, width = up_w.shape
     rows = grads.shape[1]
@@ -43,6 +43,7 @@
     has_next = sec > 0
     has_prev = sec < sections - 1
     is_last = sec == sections - 1
+    ahead = sec % 2 == 1
     full, rem = tiles_of(hid)
     wfull, wrem = tiles_of(width)
     ticks = steps // CHUNKS
@@ -168,30 +169,33 @@
             device_id_type=MESH,
         )
 
-    def out_copy(q, first, size, i):
-        span = pl.ds(first, size)
-        return pltpu.make_async_copy(moved_b.at[q, span], out_hbm.at[q, span], o_sem.at[q, i])
-
     def act_copy(tick, chunk, d):
         return spread(act, a_send, a_recv, lax.rem(tick, HELD // CHUNKS) * CHUNKS + chunk, d)
 
     def scaled_copy(chunk, d):
         return spread(scaled, s_send, s_recv, chunk, d)
 
-    def send_act(tick, chunk, reused=True):
-        if reused:
-            @pl.when(tick >= HELD // CHUNKS)
-            def _():
-                for d in range(1, n):
-                    act_copy(tick, chunk, d).wait_send()
-
+    def make_act(tick, chunk):
         _, normed = stash_rows(tick, chunk, 0, rows)
         act[lax.rem(tick, HELD // CHUNKS) * CHUNKS + chunk, me] = (normed * gain[...]).astype(jnp.bfloat16)
+
+    def start_act(tick, chunk):
         for d in range(1, n):
             act_copy(tick, chunk, d).start()
 
-    def send_scaled(chunk):
+    def send_act(tick, chunk):
+        @pl.when(tick >= HELD // CHUNKS)
+        def _():
+            for d in range(1, n):
+                act_copy(tick, chunk, d).wait_send()
+
+        make_act(tick, chunk)
+        start_act(tick, chunk)
+
+    def make_scaled(chunk):
         scaled[chunk, me] = (grads[chunk] * lscale[...]).astype(jnp.bfloat16)
+
+    def start_scaled(chunk):
         for d in range(1, n):
             scaled_copy(chunk, d).start()
 
@@ -217,7 +221,6 @@
             def _():
                 pipe_copy(steps - CHUNKS + chunk, first, size, i, True).start()
 
-            out_copy(q, first, size, i).start()
 
     def take_landed(q, chunk):
         for k in range(4):
@@ -245,21 +248,40 @@
                 pipe_copy(before, first, size, i, False).wait_recv()
             grads[chunk] = gin[before].astype(jnp.float32)
 
-        send_scaled(chunk)
+        make_scaled(chunk)
+        start_scaled(chunk)
 
     for c in range(CHUNKS):
         in_stash(c).wait()
+        make_act(0, c)
         if c == 0:
             waits = (n - 1) + has_next.astype(jnp.int32) + has_prev.astype(jnp.int32)
             pl.semaphore_wait(barrier, waits)
-        send_act(0, c, reused=False)
+
+        @pl.when(ahead)
+        def _():
+            start_act(0, c)
+
     for c in range(CHUNKS):
         in_grads(c).wait()
     load_weights()
     for c in range(CHUNKS):
-        send_scaled(c)
+        make_scaled(c)
+
+        @pl.when(ahead)
+        def _():
+            start_scaled(c)
+
+    @pl.when(jnp.logical_not(ahead))
+    def _():
+        for c in range(CHUNKS):
+            start_act(0, c)
+        for c in range(CHUNKS):
+            start_scaled(c)
+
     for c in range(CHUNKS - 1):
-        send_act(1, c, reused=False)
+        make_act(1, c)
+        start_act(1, c)
 
     @pl.when(is_last)
     def _():
@@ -368,7 +390,6 @@
 
     for q in range(steps):
         for i, (first, size) in enumerate(pieces_of(q % CHUNKS)):
-            out_copy(q, first, size, i).wait()
 
             @pl.when(has_next)
             def _():
@@ -380,6 +401,30 @@
                 part_copy(c, d, first, size, i).wait_send()
         for slot in range(min(HELD, steps)):
             act_copy(slot // CHUNKS, slot % CHUNKS, d).wait_send()
+
+
+def write_out(moved_b, pend, out_hbm, pend_hbm, wide, o_sem, e_sem):
+    steps, rows, _ = moved_b.shape
+
+    def out_copy(q):
+        return pltpu.make_async_copy(moved_b.at[q], out_hbm.at[q], o_sem.at[q])
+
+    def end_copy(c, i):
+        span = pl.ds(i * PIECE, PIECE)
+        return pltpu.make_async_copy(wide.at[c, span], pend_hbm.at[c, span], e_sem.at[c, i])
+
+    for q in range(steps):
+        out_copy(q).start()
+    for c in range(CHUNKS):
+        for i in range(rows // PIECE):
+            span = pl.ds(i * PIECE, PIECE)
+            wide[c, span] = pend[c, span].astype(jnp.float32)
+            end_copy(c, i).start()
+    for c in range(CHUNKS):
+        for i in range(rows // PIECE):
+            end_copy(c, i).wait()
+    for q in range(steps):
+        out_copy(q).wait()
 
 
 def shards(n, sections, up_weight, down_weight, norm_gain, layer_scale, stash, slot_order, received, arrivals):
@@ -396,11 +441,11 @@
     out, pend = pl.pallas_call(
         functools.partial(kernel, n, sections, steps),
         out_shape=(
-            jax.ShapeDtypeStruct((steps, rows, width), bf),
-            jax.ShapeDtypeStruct((CHUNKS, rows, width), bf),
+            pltpu.VMEM((steps, rows, width), bf),
+            pltpu.VMEM((CHUNKS, rows, width), bf),
         ),
         in_specs=[pl.BlockSpec(memory_space=pltpu.SMEM), hold, hold, far, far, far, far, far],
-        out_specs=(far, far),
+        out_specs=(hold, hold),
         scratch_shapes=[
             pltpu.VMEM((hid, width), bf),
             pltpu.VMEM((width, hid), bf),
@@ -414,7 +459,6 @@
             pltpu.VMEM((STAGES, n * rows, width), bf),
             pltpu.VMEM((CHUNKS, n - 1, rows, width), bf),
             pltpu.VMEM((steps, rows, width), bf),
-            pltpu.VMEM((steps, rows, width), bf),
             dma((tile_count,)),
             dma((STAGES,)),
             dma((2, CHUNKS)),
@@ -427,11 +471,10 @@
             dma((CHUNKS, n - 1, rows // PIECE)),
             dma((steps, rows // PIECE)),
             dma((steps, rows // PIECE)),
-            dma((steps, rows // PIECE)),
             dma((CHUNKS,)),
         ],
         compiler_params=pltpu.CompilerParams(
-            collective_id=0, has_side_effects=True, vmem_limit_bytes=67_043_328
+            collective_id=0, has_side_effects=True, vmem_limit_bytes=63_500_000
         ),
     )(
         slot_order,
@@ -443,8 +486,18 @@
         received.reshape(CHUNKS, rows, width),
         arrivals,
     )
-    pending = pend.reshape(tokens, width).astype(jnp.float32)
-    return out.reshape(1, ticks, tokens, width), pending[None]
+    emitted, pending = pl.pallas_call(
+        write_out,
+        out_shape=(
+            jax.ShapeDtypeStruct((steps, rows, width), bf),
+            jax.ShapeDtypeStruct((CHUNKS, rows, width), jnp.float32),
+        ),
+        in_specs=[hold, hold],
+        out_specs=(far, far),
+        scratch_shapes=[pltpu.VMEM((CHUNKS, rows, width), jnp.float32), dma((steps,)), dma((CHUNKS, rows // PIECE))],
+        compiler_params=pltpu.CompilerParams(vmem_limit_bytes=16_000_000),
+    )(out, pend)
+    return emitted.reshape(1, ticks, tokens, width), pending.reshape(1, tokens, width)
 
 
 def solution(mesh):

time: 175 us -> 172 us (0.983)
  other arithmetic: 2.57 us -> 0 us
    convert_element_type x1 -> x0, other arithmetic: 2.57 us -> none  [shards(): pending = pend.reshape(tokens, width).astype(jnp.float32)]
    pallas_call x0 -> x1, Pallas kernels: none -> 2.1 us  [shards(): pl.pallas_call(write_out, out_shape=(jax.ShapeDtypeStruct((steps, rows, w...]
where the time goes in v3:
time: 172 us
  Pallas kernels  171 us (99%)
    pallas_call x1, Pallas kernels, shards(): pl.pallas_call(functools.partial(kernel, n, sections, steps), out_shape=(...  169 us

profile of v3, /device:TPU:1, one launch (start us, length us, event | category | flops | bytes accessed | tf_op | source)
XLA Modules:
  0.0 171.8 jit_solution(13228939452327894756)
XLA Ops:
  0.6 169.1 %shard_map.95 = (bf16[6,64,3200]{2,1,0:T(8,128)(2,1)S(1)}, bf16[2,64,3200]{2,1,0:T(8,128)(2,1)S(1)}) custom-call(s32[1,3]{1,0:T(1,128)} %order.1, f32[1,3200]{1,0:T(1,128)} %gain.1, f32[1,3200]{1,0:T(1,128)} %lscale.1, bf16[3200,3200]{1,0:T(8,128)(2,1)} %bitcast.6, bf16[3200,3200]{1,0:T(8,128)(2,1)} %bitcast.7, bf16[3,2,64,3200]{3,2,1,0:T(8,128)(2,1)} %bitcast.8, ...), custom_call_target="tpu_custom_call" | custom-call | tf_op jit(solution)/shard_map/pallas_call | solution.py:441
  169.7 2.1 %shard_map.96 = (bf16[6,64,3200]{2,1,0:T(8,128)(2,1)}, f32[2,64,3200]{2,1,0:T(8,128)}) custom-call(bf16[6,64,3200]{2,1,0:T(8,128)(2,1)S(1)} %get-tuple-element.6.moved_b, bf16[2,64,3200]{2,1,0:T(8,128)(2,1)S(1)} %get-tuple-element.7.pend), custom_call_target="tpu_custom_call" | custom-call | tf_op jit(solution)/shard_map/pallas_call | solution.py:489

commit v4 on v3

--- a/solution.py
+++ b/solution.py
@@ -31,10 +31,10 @@
 
 
 def kernel(
-    n, sections, steps, order, gain, lscale, up_hbm, down_hbm, stash_hbm, received_hbm, arrivals_hbm,
+    n, sections, steps, order_hbm, gain_hbm, lscale_hbm, up_hbm, down_hbm, stash_hbm, received_hbm, arrivals_hbm,
     moved_b, pend_hbm,
-    up_w, down_t, stash0, stash1, grads, act, scaled, factor_of, slope, psend, precv, gin,
-    wsem, tsem, isem, l_sem, a_send, a_recv, s_send, s_recv, p_send, p_recv, g_send, g_recv, e_sem,
+    order, gain, lscale, up_w, down_t, stash0, stash1, grads, act, scaled, factor_of, slope, psend, precv, gin,
+    wsem, tsem, isem, v_sem, l_sem, a_send, a_recv, s_send, s_recv, p_send, p_recv, g_send, g_recv, e_sem, hand_sem,
 ):
     hid, width = up_w.shape
     rows = grads.shape[1]
@@ -43,7 +43,7 @@
     has_next = sec > 0
     has_prev = sec < sections - 1
     is_last = sec == sections - 1
-    ahead = sec % 2 == 1
+    leads = sec % 2 == 0
     full, rem = tiles_of(hid)
     wfull, wrem = tiles_of(width)
     ticks = steps // CHUNKS
@@ -62,13 +62,32 @@
     def rows_at(device, first, size):
         return pl.ds(pl.multiple_of(device * rows + first, PIECE if first else size), size)
 
+    barrier = pltpu.get_barrier_semaphore()
+    for d in range(1, n):
+        pl.semaphore_signal(barrier, inc=1, device_id={"tensor": peer(d)}, device_id_type=MESH)
+
+    @pl.when(has_next)
+    def _():
+        pl.semaphore_signal(barrier, inc=1, device_id={"pipe": sec - 1}, device_id_type=MESH)
+
+    @pl.when(has_prev)
+    def _():
+        pl.semaphore_signal(barrier, inc=1, device_id={"pipe": sec + 1}, device_id_type=MESH)
+
     def in_stash(c):
         return pltpu.make_async_copy(stash_hbm.at[:, c], stash[c], isem.at[0, c])
 
     def in_grads(c):
         return pltpu.make_async_copy(received_hbm.at[c], grads.at[c], isem.at[1, c])
 
-    for c in range(CHUNKS):
+    in_order = pltpu.make_async_copy(order_hbm, order, v_sem.at[0])
+    in_gain = pltpu.make_async_copy(gain_hbm, gain, v_sem.at[1])
+    in_lscale = pltpu.make_async_copy(lscale_hbm, lscale, v_sem.at[2])
+    in_order.start()
+    in_gain.start()
+    in_stash(0).start()
+    in_lscale.start()
+    for c in range(1, CHUNKS):
         in_stash(c).start()
     for c in range(CHUNKS):
         in_grads(c).start()
@@ -121,18 +140,6 @@
             l_sem.at[q, k],
         )
 
-    barrier = pltpu.get_barrier_semaphore()
-    for d in range(1, n):
-        pl.semaphore_signal(barrier, inc=1, device_id={"tensor": peer(d)}, device_id_type=MESH)
-
-    @pl.when(has_next)
-    def _():
-        pl.semaphore_signal(barrier, inc=1, device_id={"pipe": sec - 1}, device_id_type=MESH)
-
-    @pl.when(has_prev)
-    def _():
-        pl.semaphore_signal(barrier, inc=1, device_id={"pipe": sec + 1}, device_id_type=MESH)
-
     def stash_rows(tick, chunk, first, size):
         values = stash[chunk][order[0, tick], pl.ds(first, size)].astype(jnp.float32)
         factor = lax.rsqrt(jnp.mean(values * values, axis=-1, keepdims=True) + EPS)
@@ -221,6 +228,23 @@
             def _():
                 pipe_copy(steps - CHUNKS + chunk, first, size, i, True).start()
 
+            if chunk == CHUNKS - 1 and i == 0:
+                pl.when(leads & jnp.logical_not(more))(hand_over)
+
+
+    def start_pieces():
+        for i, (first, size) in enumerate(pieces):
+            for d in range(1, n):
+                part_copy(CHUNKS - 1, d, first, size, i).start()
+
+    def sent_pieces():
+        for i, (first, size) in enumerate(pieces[:-1]):
+            for d in range(1, n):
+                part_copy(CHUNKS - 1, d, first, size, i).wait_send()
+
+    def hand_over():
+        sent_pieces()
+        pl.semaphore_signal(hand_sem, inc=1, device_id={"pipe": sec + 1}, device_id_type=MESH)
 
     def take_landed(q, chunk):
         for k in range(4):
@@ -251,6 +275,8 @@
         make_scaled(chunk)
         start_scaled(chunk)
 
+    in_order.wait()
+    in_gain.wait()
     for c in range(CHUNKS):
         in_stash(c).wait()
         make_act(0, c)
@@ -258,26 +284,16 @@
             waits = (n - 1) + has_next.astype(jnp.int32) + has_prev.astype(jnp.int32)
             pl.semaphore_wait(barrier, waits)
 
-        @pl.when(ahead)
-        def _():
-            start_act(0, c)
-
+        start_act(0, c)
+
+    in_lscale.wait()
     for c in range(CHUNKS):
         in_grads(c).wait()
     load_weights()
     for c in range(CHUNKS):
         make_scaled(c)
 
-        @pl.when(ahead)
-        def _():
-            start_scaled(c)
-
-    @pl.when(jnp.logical_not(ahead))
-    def _():
-        for c in range(CHUNKS):
-            start_act(0, c)
-        for c in range(CHUNKS):
-            start_scaled(c)
+        start_scaled(c)
 
     for c in range(CHUNKS - 1):
         make_act(1, c)
@@ -310,6 +326,11 @@
             hidden_tile(full, rem)
 
         for c in range(CHUNKS):
+            if c == CHUNKS - 1:
+                @pl.when(more)
+                def _():
+                    send_act(tick + 1, CHUNKS - 1)
+
             for d in range(1, n):
                 scaled_copy(c, d).wait_recv()
 
@@ -342,15 +363,15 @@
             if wrem:
                 down_tile(wfull, wrem)
             if c == CHUNKS - 1:
-                for i, (first, size) in enumerate(pieces_of(c)):
-                    for d in range(1, n):
-                        part_copy(c, d, first, size, i).start()
-
-        @pl.when(more)
-        def _():
-            send_act(tick + 1, CHUNKS - 1)
-
-        for c in range(CHUNKS):
+                pl.when(more | leads)(start_pieces)
+
+        for c in range(CHUNKS):
+            if c == CHUNKS - 1:
+                @pl.when(jnp.logical_not(more | leads))
+                def _():
+                    pl.semaphore_wait(hand_sem, 1)
+                    start_pieces()
+
             finish(tick, c, more)
 
             @pl.when(more)
@@ -395,10 +416,11 @@
             def _():
                 pipe_copy(q, first, size, i, q >= steps - CHUNKS).wait_send()
 
+    pl.when(jnp.logical_not(leads))(sent_pieces)
     for d in range(1, n):
         for c in range(CHUNKS):
-            for i, (first, size) in enumerate(pieces_of(c)):
-                part_copy(c, d, first, size, i).wait_send()
+            first, size = pieces_of(c)[-1]
+            part_copy(c, d, first, size, len(pieces_of(c)) - 1).wait_send()
         for slot in range(min(HELD, steps)):
             act_copy(slot // CHUNKS, slot % CHUNKS, d).wait_send()
 
@@ -444,9 +466,12 @@
             pltpu.VMEM((steps, rows, width), bf),
             pltpu.VMEM((CHUNKS, rows, width), bf),
         ),
-        in_specs=[pl.BlockSpec(memory_space=pltpu.SMEM), hold, hold, far, far, far, far, far],
+        in_specs=[far] * 8,
         out_specs=(hold, hold),
         scratch_shapes=[
+            pltpu.SMEM(slot_order.shape, jnp.int32),
+            pltpu.VMEM(norm_gain.shape, jnp.float32),
+            pltpu.VMEM(layer_scale.shape, jnp.float32),
             pltpu.VMEM((hid, width), bf),
             pltpu.VMEM((width, hid), bf),
             pltpu.VMEM((ticks, rows, width), bf),
@@ -462,6 +487,7 @@
             dma((tile_count,)),
             dma((STAGES,)),
             dma((2, CHUNKS)),
+            dma((3,)),
             dma((steps, 4)),
             dma((HELD, n - 1)),
             dma((HELD, n - 1)),
@@ -472,6 +498,7 @@
             dma((steps, rows // PIECE)),
             dma((steps, rows // PIECE)),
             dma((CHUNKS,)),
+            pltpu.SemaphoreType.REGULAR,
         ],
         compiler_params=pltpu.CompilerParams(
             collective_id=0, has_side_effects=True, vmem_limit_bytes=63_500_000

time: 172 us -> 170 us (0.988)
  Pallas kernels: 171 us -> 169 us
    pallas_call x1, Pallas kernels: 169 us -> 167 us  [shards(): pl.pallas_call(functools.partial(kernel, n, sections, steps), out_shape=(...]
where the time goes in v4:
time: 170 us
  Pallas kernels  169 us (99%)
    pallas_call x1, Pallas kernels, shards(): pl.pallas_call(functools.partial(kernel, n, sections, steps), out_shape=(...  167 us

profile of v4, /device:TPU:1, one launch (start us, length us, event | category | flops | bytes accessed | tf_op | source)
XLA Modules:
  0.0 170.0 jit_solution(16294698419245085638)
XLA Ops:
  0.6 167.2 %shard_map.95 = (bf16[6,64,3200]{2,1,0:T(8,128)(2,1)S(1)}, bf16[2,64,3200]{2,1,0:T(8,128)(2,1)S(1)}) custom-call(s32[1,3]{1,0:T(1,128)} %order_hbm.1, f32[1,3200]{1,0:T(1,128)} %gain_hbm.1, f32[1,3200]{1,0:T(1,128)} %lscale_hbm.1, bf16[3200,3200]{1,0:T(8,128)(2,1)} %bitcast.6, bf16[3200,3200]{1,0:T(8,128)(2,1)} %bitcast.7, bf16[3,2,64,3200]{3,2,1,0:T(8,128)(2,1)} %bitcast.8, ...), custom_call_target="tpu_custom_call" | custom-call | tf_op jit(solution)/shard_map/pallas_call | solution.py:463
  167.9 2.1 %shard_map.96 = (bf16[6,64,3200]{2,1,0:T(8,128)(2,1)}, f32[2,64,3200]{2,1,0:T(8,128)}) custom-call(bf16[6,64,3200]{2,1,0:T(8,128)(2,1)S(1)} %get-tuple-element.6.moved_b, bf16[2,64,3200]{2,1,0:T(8,128)(2,1)S(1)} %get-tuple-element.7.pend), custom_call_target="tpu_custom_call" | custom-call | tf_op jit(solution)/shard_map/pallas_call | solution.py:516

commit v5 on v4

--- a/solution.py
+++ b/solution.py
@@ -238,7 +238,7 @@
                 part_copy(CHUNKS - 1, d, first, size, i).start()
 
     def sent_pieces():
-        for i, (first, size) in enumerate(pieces[:-1]):
+        for i, (first, size) in enumerate(pieces[:-2]):
             for d in range(1, n):
                 part_copy(CHUNKS - 1, d, first, size, i).wait_send()
 
@@ -419,8 +419,9 @@
     pl.when(jnp.logical_not(leads))(sent_pieces)
     for d in range(1, n):
         for c in range(CHUNKS):
-            first, size = pieces_of(c)[-1]
-            part_copy(c, d, first, size, len(pieces_of(c)) - 1).wait_send()
+            for i, (first, size) in enumerate(pieces_of(c)):
+                if i >= len(pieces_of(c)) - 2:
+                    part_copy(c, d, first, size, i).wait_send()
         for slot in range(min(HELD, steps)):
             act_copy(slot // CHUNKS, slot % CHUNKS, d).wait_send()
 
@@ -435,13 +436,13 @@
         span = pl.ds(i * PIECE, PIECE)
         return pltpu.make_async_copy(wide.at[c, span], pend_hbm.at[c, span], e_sem.at[c, i])
 
-    for q in range(steps):
-        out_copy(q).start()
     for c in range(CHUNKS):
         for i in range(rows // PIECE):
             span = pl.ds(i * PIECE, PIECE)
             wide[c, span] = pend[c, span].astype(jnp.float32)
             end_copy(c, i).start()
+    for q in range(steps):
+        out_copy(q).start()
     for c in range(CHUNKS):
         for i in range(rows // PIECE):
             end_copy(c, i).wait()

time: 170 us -> 170 us (level)
  no operation moved by 1% of the time
where the time goes in v5:
time: 170 us
  Pallas kernels  169 us (99%)
    pallas_call x1, Pallas kernels, shards(): pl.pallas_call(functools.partial(kernel, n, sections, steps), out_shape=(...  167 us

profile of v5, /device:TPU:1, one launch (start us, length us, event | category | flops | bytes accessed | tf_op | source)
XLA Modules:
  0.0 170.0 jit_solution(6787956672252164259)
XLA Ops:
  0.6 167.2 %shard_map.95 = (bf16[6,64,3200]{2,1,0:T(8,128)(2,1)S(1)}, bf16[2,64,3200]{2,1,0:T(8,128)(2,1)S(1)}) custom-call(s32[1,3]{1,0:T(1,128)} %order_hbm.1, f32[1,3200]{1,0:T(1,128)} %gain_hbm.1, f32[1,3200]{1,0:T(1,128)} %lscale_hbm.1, bf16[3200,3200]{1,0:T(8,128)(2,1)} %bitcast.6, bf16[3200,3200]{1,0:T(8,128)(2,1)} %bitcast.7, bf16[3,2,64,3200]{3,2,1,0:T(8,128)(2,1)} %bitcast.8, ...), custom_call_target="tpu_custom_call" | custom-call | tf_op jit(solution)/shard_map/pallas_call | solution.py:464
  167.9 2.1 %shard_map.96 = (bf16[6,64,3200]{2,1,0:T(8,128)(2,1)}, f32[2,64,3200]{2,1,0:T(8,128)}) custom-call(bf16[6,64,3200]{2,1,0:T(8,128)(2,1)S(1)} %get-tuple-element.6.moved_b, bf16[2,64,3200]{2,1,0:T(8,128)(2,1)S(1)} %get-tuple-element.7.pend), custom_call_target="tpu_custom_call" | custom-call | tf_op jit(solution)/shard_map/pallas_call | solution.py:517
